TPU v7x, 32 devices: a whole 2x2x4 slice. The times are simulated.
32 devices in a mesh: layer: 2 (over core), prow: 4 (over z), pcol: 4 (over y, x).
Axes of the slice: x: 2, y: 2, z: 4, core: 2. Of those that a mesh axis runs over, the one named last changes fastest.
Arguments:
- factor: bfloat16 [2, 4, 4, 4, 4, 256, 256], P('layer', 'prow', None, None, 'pcol'), may hold values from -0.1875 to 0.1875
- factor_scale: float32 [2, 4, 4, 4, 4], P('layer', 'prow', None, None, 'pcol'), may hold values from 0.25 to 4
- sub_pattern: int32 [2, 4, 4, 4, 4], P('layer', 'prow', None, None, 'pcol'), may hold values from 0 to 1, as said below
- coupling: bfloat16 [2, 4, 4, 4, 4, 256, 256], P('layer', 'prow', None, None, 'pcol'), may hold values from -0.1875 to 0.1875
- coupling_scale: float32 [2, 4, 4, 4, 4], P('layer', 'prow', None, None, 'pcol'), may hold values from 0.25 to 4
- top_pattern: int32 [2, 4, 4, 4, 4], P('layer', 'prow', None, None, 'pcol'), may hold values 0 or 1
- diag_inverse: float32 [2, 4, 4, 256, 256], P('layer', 'prow', 'pcol'), may hold values from -1 to 2
- top_inverse: float32 [4, 4, 256, 256], P('prow', 'pcol'), may hold values from -1 to 2
- rhs_sub: float32 [2, 4, 4, 256, 256], P('layer', 'prow', 'pcol'), may hold values from -6 to 6
- rhs_top: float32 [4, 4, 256, 256], P('prow', 'pcol'), may hold values from -6 to 6
Outputs:
- sol_sub: float32 [2, 4, 4, 256, 256], P('layer', 'prow', 'pcol')
- sol_top: float32 [4, 4, 256, 256], P('prow', 'pcol')
Inputs may be any that keep to these rules, and one draw needn't show every extreme that they name: The supernodes of each layer fall into 3 levels; sub_pattern is 1 only where the column supernode's level is below the row supernode's level.
All inputs are finite; a program needn't handle non-finite values. No bound on the sum of `top_pattern` on one device may be relied on, other than what follows from the above.
Results may differ from a plain program's by a relative error of at most 0.02.
Values may be sent and summed in bfloat16 or wider, within the bound.
No kernel may reach another device: no remote copies, remote signals or barrier semaphores. Data moves between devices by JAX's collectives and lax.ppermute only.
A program may use at most 64 MiB of HBM per device.

v0:
```python
import jax
import jax.numpy as jnp
from jax import lax
from jax.sharding import PartitionSpec as P

LEVELS = 3
HIGH_PREC = lax.Precision.HIGHEST


def apply_left(matrix, values):
    return jnp.dot(matrix, values, precision=HIGH_PREC, preferred_element_type=jnp.float32)


def apply_trans(matrix, values):
    return jnp.dot(matrix.T, values, precision=HIGH_PREC, preferred_element_type=jnp.float32)


def forward_partial(values, matrices, scaling):
    shared = values.astype(jnp.bfloat16)[None]
    products = jnp.einsum(
        "bawk,akr->bawr",
        matrices,
        lax.all_gather(shared, "prow", axis=0, tiled=True),
        preferred_element_type=jnp.float32,
    )
    return jnp.sum(products * scaling[:, :, None, None], axis=1)


def column_total(values, matrices, scaling):
    shared = values.astype(jnp.bfloat16)[None]
    products = jnp.einsum(
        "bakw,bkr->bawr",
        matrices,
        lax.all_gather(shared, "pcol", axis=0, tiled=True),
        preferred_element_type=jnp.float32,
    )
    partial_value = jnp.sum(products * scaling[:, :, None, None], axis=0)
    return lax.psum_scatter(
        partial_value.astype(jnp.bfloat16), "prow", scatter_dimension=0, tiled=True
    ).astype(jnp.float32)[0]


def shards(
    factor,
    factor_scale,
    sub_pattern,
    coupling,
    coupling_scale,
    top_pattern,
    diag_inverse,
    top_inverse,
    rhs_sub,
    rhs_top,
):
    super_width = factor.shape[5]
    row_count = factor.shape[2]
    col_count = factor.shape[3]
    factor_blocks = factor.reshape(row_count, col_count, super_width, super_width)
    factor_weights = (factor_scale * sub_pattern.astype(jnp.float32)).reshape(row_count, col_count)
    link_blocks = coupling.reshape(row_count, col_count, super_width, super_width)
    link_weights = (coupling_scale * top_pattern.astype(jnp.float32)).reshape(row_count, col_count)
    inverse = diag_inverse.reshape(super_width, super_width)
    top_matrix = top_inverse.reshape(super_width, super_width)
    own_rhs = rhs_sub.reshape(super_width, rhs_sub.shape[-1])
    top_rhs = rhs_top.reshape(super_width, rhs_top.shape[-1])
    solved = apply_left(inverse, own_rhs)
    for sweep_index in range(LEVELS - 1):
        partial_value = forward_partial(solved, factor_blocks, factor_weights)
        lower_sum = lax.psum_scatter(
            partial_value.astype(jnp.bfloat16), "pcol", scatter_dimension=0, tiled=True
        ).astype(jnp.float32)[0]
        solved = apply_left(inverse, own_rhs - lower_sum)
    top_partial = forward_partial(solved, link_blocks, link_weights)
    top_part = lax.psum_scatter(
        top_partial.astype(jnp.bfloat16), "pcol", scatter_dimension=0, tiled=True
    ).astype(jnp.float32)[0]
    merged = lax.psum(top_part.astype(jnp.bfloat16), "layer").astype(jnp.float32)
    top_fwd = apply_left(top_matrix, top_rhs - merged)
    top_answer = apply_trans(top_matrix, top_fwd)
    coupled = column_total(top_answer, link_blocks, link_weights)
    answer = apply_trans(inverse, solved - coupled)
    for sweep_index in range(LEVELS - 1):
        upper_sum = column_total(answer, factor_blocks, factor_weights)
        answer = apply_trans(inverse, solved - coupled - upper_sum)
    return (answer.reshape(rhs_sub.shape), top_answer.reshape(rhs_top.shape))


def solution(mesh):
    return jax.shard_map(
        shards,
        mesh=mesh,
        in_specs=(
            P("layer", "prow", None, None, "pcol", None, None),
            P("layer", "prow", None, None, "pcol"),
            P("layer", "prow", None, None, "pcol"),
            P("layer", "prow", None, None, "pcol", None, None),
            P("layer", "prow", None, None, "pcol"),
            P("layer", "prow", None, None, "pcol"),
            P("layer", "prow", "pcol", None, None),
            P("prow", "pcol", None, None),
            P("layer", "prow", "pcol", None, None),
            P("prow", "pcol", None, None),
        ),
        out_specs=(P("layer", "prow", "pcol", None, None), P("prow", "pcol", None, None)),
        check_vma=False,
    )
```

profile of v0, /device:TPU:0, one launch (start us, length us, event | category | flops | bytes accessed | tf_op | source)
XLA Modules:
  0.0 298.1 jit_solution(12780264937894898415)
XLA Ops:
  8.2 1.4 convolution_convert_fusion.3
  9.6 17.4 %all-gather = bf16[1024,256]{1,0:T(8,128)(2,1)S(1)} all-gather(bf16[256,256]{1,0:T(8,128)(2,1)S(1)} %convolution_convert_fusion.3), channel_id=2, replica_groups=mesh['layer'=2,'prow'=4,'pcol'=4] {'prow'}, dimensions={0}, use_global_device_ids=true | all-gather | bytes 655360 | tf_op jit(solution)/shard_map/all_gather | solution.py:23
  28.9 27.0 %reduce-scatter.19.cloned.1.call-done = bf16[1,256,256]{2,1,0:T(8,128)(2,1)} async-done(((bf16[4,256,256]{2,1,0:T(8,128)(2,1)}), bf16[1,256,256]{2,1,0:T(8,128)(2,1)}) %reduce-scatter.19.cloned.1.call-update) | async-done | bytes 131088
  55.9 1.5 fusion.6
  57.4 15.4 %all-gather.1 = bf16[1024,256]{0,1:T(8,128)(2,1)S(1)} all-gather(bf16[256,256]{0,1:T(8,128)(2,1)S(1)} %fusion.6), channel_id=3, replica_groups=mesh['layer'=2,'prow'=4,'pcol'=4] {'prow'}, dimensions={0}, use_global_device_ids=true | all-gather | bytes 655360 | tf_op jit(solution)/shard_map/all_gather | solution.py:23
  74.0 1.9 fusion.1
  77.0 25.9 %reduce-scatter.21.cloned.1.call-done = bf16[1,256,256]{2,1,0:T(8,128)(2,1)} async-done(((bf16[4,256,256]{2,1,0:T(8,128)(2,1)}), bf16[1,256,256]{2,1,0:T(8,128)(2,1)}) %reduce-scatter.21.cloned.1.call-update) | async-done | bytes 131088
  102.9 1.5 fusion.37
  104.4 15.4 %all-gather.2 = bf16[1024,256]{0,1:T(8,128)(2,1)S(1)} all-gather(bf16[256,256]{0,1:T(8,128)(2,1)S(1)} %get-tuple-element.6), channel_id=4, replica_groups=mesh['layer'=2,'prow'=4,'pcol'=4] {'prow'}, dimensions={0}, use_global_device_ids=true | all-gather | bytes 655360 | tf_op jit(solution)/shard_map/all_gather | solution.py:23
  121.0 3.5 %fusion = bf16[4,256,256]{1,2,0:T(8,128)(2,1)} fusion(f32[4,4]{0,1:T(4,128)S(1)} %copy.34, bf16[4,256,256,1]{1,0,2,3:T(4,128)(2,1)} %bitcast.158, bf16[1,1,4,4,1,256,256]{6,5,4,3,2,1,0:T(8,128)(2,1)} %param.13), kind=kOutput, calls=%fused_computation.1 | convolution fusion | flops 538705920 | bytes 3145792 | tf_op jit(solution)/shard_map/bawk,akr->bawr/dot_general | solution.py:20
  124.5 2.1 copy.35
  126.6 26.0 %reduce-scatter.23.cloned.1.call-done = bf16[1,256,256]{2,1,0:T(8,128)(2,1)} async-done(((bf16[4,256,256]{2,1,0:T(8,128)(2,1)}), bf16[1,256,256]{2,1,0:T(8,128)(2,1)}) %reduce-scatter.23.cloned.1.call-update) | async-done | bytes 131088
  152.7 20.1 %all-reduce.5.cloned.1.call-done = bf16[256,256]{1,0:T(8,128)(2,1)} async-done(((bf16[256,256]{1,0:T(8,128)(2,1)}), bf16[256,256]{1,0:T(8,128)(2,1)}) %all-reduce.5.cloned.1.call-update) | async-done | bytes 131088 | tf_op jit(solution)/shard_map/psum | solution.py:77
  172.7 1.5 fusion.20
  174.6 14.6 %all-gather.3 = bf16[1024,256]{0,1:T(8,128)(2,1)S(1)} all-gather(bf16[256,256]{0,1:T(8,128)(2,1)S(1)} %get-tuple-element.8), channel_id=5, replica_groups=mesh['layer'=2,'prow'=4,'pcol'=4] {'pcol'}, dimensions={0}, use_global_device_ids=true | all-gather | bytes 655360 | tf_op jit(solution)/shard_map/all_gather | solution.py:34
  190.4 3.4 %multiply_reduce_fusion.2 = bf16[256,4,256]{2,0,1:T(8,128)(2,1)} fusion(f32[4,4]{1,0:T(4,128)S(1)} %bitcast.167, bf16[4,256,256,1]{1,0,2,3:T(4,128)(2,1)} %bitcast.159, bf16[1,1,4,4,1,256,256]{6,5,4,3,2,1,0:T(8,128)(2,1)} %param.13), kind=kOutput, calls=%fused_computation.8 | convolution fusion | flops 538705920 | bytes 3145792 | tf_op jit(solution)/shard_map/bakw,bkr->bawr/dot_general | solution.py:31
  193.9 22.0 %reduce-scatter.13.cloned.1.call-done = bf16[1,256,256]{1,2,0:T(8,128)(2,1)} async-done(((bf16[4,256,256]{1,2,0:T(8,128)(2,1)}), bf16[1,256,256]{1,2,0:T(8,128)(2,1)}) %reduce-scatter.13.cloned.1.call-update) | async-done | bytes 131088 | tf_op jit(solution)/shard_map/reduce_scatter | solution.py:38
  217.1 12.0 %all-gather.4 = bf16[1024,256]{0,1:T(8,128)(2,1)S(1)} all-gather(bf16[256,256]{0,1:T(8,128)(2,1)S(1)} %fusion.7), channel_id=6, replica_groups=mesh['layer'=2,'prow'=4,'pcol'=4] {'pcol'}, dimensions={0}, use_global_device_ids=true | all-gather | bytes 655360 | tf_op jit(solution)/shard_map/all_gather | solution.py:34
  230.3 2.7 multiply_reduce_fusion.1
  233.1 19.4 %reduce-scatter.15.cloned.1.call-done = bf16[1,256,256]{1,2,0:T(8,128)(2,1)} async-done(((bf16[4,256,256]{1,2,0:T(8,128)(2,1)}), bf16[1,256,256]{1,2,0:T(8,128)(2,1)}) %reduce-scatter.15.cloned.1.call-update) | async-done | bytes 131088 | tf_op jit(solution)/shard_map/reduce_scatter | solution.py:38
  252.4 1.3 fusion.8
  253.7 12.0 %all-gather.5 = bf16[1024,256]{0,1:T(8,128)(2,1)S(1)} all-gather(bf16[256,256]{0,1:T(8,128)(2,1)S(1)} %fusion.8), channel_id=7, replica_groups=mesh['layer'=2,'prow'=4,'pcol'=4] {'pcol'}, dimensions={0}, use_global_device_ids=true | all-gather | bytes 655360 | tf_op jit(solution)/shard_map/all_gather | solution.py:34
  267.0 2.7 multiply_reduce_fusion
  270.5 18.6 %reduce-scatter.17.cloned.1.call-done = bf16[1,256,256]{1,2,0:T(8,128)(2,1)} async-done(((bf16[4,256,256]{1,2,0:T(8,128)(2,1)}), bf16[1,256,256]{1,2,0:T(8,128)(2,1)}) %reduce-scatter.17.cloned.1.call-update) | async-done | bytes 131088 | tf_op jit(solution)/shard_map/reduce_scatter | solution.py:38
  (47 shorter events, 14.9 us)
Async XLA Ops:
  7.2 19.8 %copy-start = (bf16[1,1,4,4,1,256,256]{6,5,4,3,2,1,0:T(8,128)(2,1)S(1)}, bf16[1,1,4,4,1,256,256]{6,5,4,3,2,1,0:T(8,128)(2,1)}, u32[]{:S(2)}) copy-start(bf16[1,1,4,4,1,256,256]{6,5,4,3,2,1,0:T(8,128)(2,1)} %param.10) | copy-start | bytes 6291460
  7.2 48.7 %reduce-scatter.19.cloned.1.call-start = ((), (), s32[]{:S(2)}) async-start(), calls=%async_computation.10 | async-start | bytes 655360
  27.0 29.0 %copy-start.1 = (f32[1,1,1,256,256]{4,3,2,1,0:T(8,128)S(1)}, f32[1,1,1,256,256]{4,3,2,1,0:T(8,128)}, u32[]{:S(2)}) copy-start(f32[1,1,1,256,256]{4,3,2,1,0:T(8,128)} %param.16) | copy-start | bytes 786436
  27.0 29.0 %copy-start.2 = (f32[1,1,1,256,256]{4,3,2,1,0:T(8,128)S(1)}, f32[1,1,1,256,256]{4,3,2,1,0:T(8,128)}, u32[]{:S(2)}) copy-start(f32[1,1,1,256,256]{4,3,2,1,0:T(8,128)} %param.18) | copy-start | bytes 786436
  28.9 74.0 %reduce-scatter.21.cloned.1.call-start = ((), (), s32[]{:S(2)}) async-start(), calls=%async_computation.11 | async-start | bytes 655360
  74.0 2.9 copy-start.6
  74.0 3.0 copy-start.7
  76.9 75.7 %reduce-scatter.23.cloned.1.call-start = ((), (), s32[]{:S(2)}) async-start(), calls=%async_computation.12 | async-start | bytes 655360
  121.0 51.7 %copy-start.4 = (f32[1,1,256,256]{3,2,1,0:T(8,128)S(1)}, f32[1,1,256,256]{3,2,1,0:T(8,128)}, u32[]{:S(2)}) copy-start(f32[1,1,256,256]{3,2,1,0:T(8,128)} %param.17) | copy-start | bytes 786436
  121.0 51.7 %copy-start.5 = (f32[1,1,256,256]{3,2,1,0:T(8,128)S(1)}, f32[1,1,256,256]{3,2,1,0:T(8,128)}, u32[]{:S(2)}) copy-start(f32[1,1,256,256]{3,2,1,0:T(8,128)} %param.19) | copy-start | bytes 786436
  126.5 46.2 %all-reduce.5.cloned.1.call-start = ((), (), s32[]{:S(2)}) async-start(), calls=%async_computation.6 | async-start | bytes 262144 | tf_op jit(solution)/shard_map/psum | solution.py:77
  152.6 63.2 %reduce-scatter.13.cloned.1.call-start = ((), (), s32[]{:S(2)}) async-start(), calls=%async_computation.7 | async-start | bytes 655360 | tf_op jit(solution)/shard_map/reduce_scatter | solution.py:38
  193.8 58.6 %reduce-scatter.15.cloned.1.call-start = ((), (), s32[]{:S(2)}) async-start(), calls=%async_computation.8 | async-start | bytes 655360 | tf_op jit(solution)/shard_map/reduce_scatter | solution.py:38
  230.3 22.1 %copy-start.3 = (bf16[1,256,256]{1,2,0:T(8,128)(2,1)S(1)}, bf16[1,256,256]{1,2,0:T(8,128)(2,1)}, u32[]{:S(2)}) copy-start(bf16[1,256,256]{1,2,0:T(8,128)(2,1)} %reduce-scatter.13.cloned.1.call-done) | copy-start | bytes 393220
  233.0 56.1 %reduce-scatter.17.cloned.1.call-start = ((), (), s32[]{:S(2)}) async-start(), calls=%async_computation.9 | async-start | bytes 655360 | tf_op jit(solution)/shard_map/reduce_scatter | solution.py:38
Sparse Core Ops, SparseCore 0:
  29.0 26.8 reduce-scatter.18
  77.0 25.8 reduce-scatter.20
  126.7 25.8 reduce-scatter.22
  154.7 17.9 all-reduce.4
  193.9 21.8 reduce-scatter.12
  233.1 19.2 reduce-scatter.14
  269.8 19.2 reduce-scatter.16
where the time goes:
time: 299 us; the launch traced here: 298 us
  waiting for transfers between devices  159 us (53%)
  blocking collectives  86.8 us (29%)
  matrix products  25.1 us (8%)
  between operations  14.2 us (5%)
  local copies, waits for them, and re-layouts  11.8 us (4%)
    unnamed x10, waiting for transfers between devices  78.9 us
    reduce_scatter x3, waiting for transfers between devices, column_total(): lax.psum_scatter(partial_value.astype(jnp.bfloat16), 'prow', scatter_dime...  59.9 us
    all_gather x3, blocking collectives, forward_partial(): lax.all_gather(shared, 'prow', axis=0, tiled=True)  48.2 us
    all_gather x3, blocking collectives, column_total(): lax.all_gather(shared, 'pcol', axis=0, tiled=True)  38.7 us
    psum x1, waiting for transfers between devices, shards(): lax.psum(top_part.astype(jnp.bfloat16), 'layer').astype(jnp.float32)  20.1 us
    dot_general x3, matrix products, column_total(): jnp.einsum('bakw,bkr->bawr', matrices, lax.all_gather(shared, 'pcol', axi...  8.74 us
    dot_general x3, matrix products, forward_partial(): jnp.einsum('bawk,akr->bawr', matrices, lax.all_gather(shared, 'prow', axi...  6.24 us
  transfers between devices with their start and end apart: 7, of which 7 were waited for; matrix products, arithmetic and copies ran while one was open for 0% of the time, Pallas kernels for 0%

commit v1 on v0

--- a/solution.py
+++ b/solution.py
@@ -74,7 +74,9 @@
     top_part = lax.psum_scatter(
         top_partial.astype(jnp.bfloat16), "pcol", scatter_dimension=0, tiled=True
     ).astype(jnp.float32)[0]
-    merged = lax.psum(top_part.astype(jnp.bfloat16), "layer").astype(jnp.float32)
+    merged = jnp.sum(lax.all_gather(top_part.astype(jnp.bfloat16), "layer"), axis=0).astype(
+        jnp.float32
+    )
     top_fwd = apply_left(top_matrix, top_rhs - merged)
     top_answer = apply_trans(top_matrix, top_fwd)
     coupled = column_total(top_answer, link_blocks, link_weights)

time: 299 us -> 279 us (0.933)
  waiting for transfers between devices: 159 us -> 139 us
    psum x1 -> x0, waiting for transfers between devices: 20.1 us -> none  [shards(): lax.psum(top_part.astype(jnp.bfloat16), 'layer').astype(jnp.float32)]
    unnamed x10 -> x9, waiting for transfers between devices: 78.9 us -> 78.9 us
  transfers between devices with their start and end apart: 7 -> 6, of which waited for: 7 -> 6; matrix products, arithmetic and copies ran while one was open for 0% -> 0% of each run, Pallas kernels for 0% -> 0%
where the time goes in v1:
time: 279 us
  waiting for transfers between devices  139 us (50%)
  blocking collectives  88.5 us (32%)
  matrix products  24.2 us (9%)
  between operations  14.2 us (5%)
  local copies, waits for them, and re-layouts  11.9 us (4%)
    unnamed x9, waiting for transfers between devices  78.9 us
    reduce_scatter x3, waiting for transfers between devices, column_total(): lax.psum_scatter(partial_value.astype(jnp.bfloat16), 'prow', scatter_dime...  59.9 us
    all_gather x3, blocking collectives, forward_partial(): lax.all_gather(shared, 'prow', axis=0, tiled=True)  48.2 us
    all_gather x3, blocking collectives, column_total(): lax.all_gather(shared, 'pcol', axis=0, tiled=True)  38.2 us
    dot_general x3, matrix products, column_total(): jnp.einsum('bakw,bkr->bawr', matrices, lax.all_gather(shared, 'pcol', axi...  8.74 us
    dot_general x3, matrix products, forward_partial(): jnp.einsum('bawk,akr->bawr', matrices, lax.all_gather(shared, 'prow', axi...  6.21 us
  transfers between devices with their start and end apart: 6, of which 6 were waited for; matrix products, arithmetic and copies ran while one was open for 0% of the time, Pallas kernels for 0%

profile of v1, /device:TPU:0, one launch (start us, length us, event | category | flops | bytes accessed | tf_op | source)
XLA Modules:
  0.0 278.8 jit_solution(9389369926255821906)
XLA Ops:
  8.2 1.4 convolution_convert_fusion.3
  9.6 17.4 %all-gather = bf16[1024,256]{1,0:T(8,128)(2,1)S(1)} all-gather(bf16[256,256]{1,0:T(8,128)(2,1)S(1)} %convolution_convert_fusion.3), channel_id=2, replica_groups=mesh['layer'=2,'prow'=4,'pcol'=4] {'prow'}, dimensions={0}, use_global_device_ids=true | all-gather | bytes 655360 | tf_op jit(solution)/shard_map/all_gather | solution.py:23
  28.9 27.0 %reduce-scatter.19.cloned.1.call-done = bf16[1,256,256]{2,1,0:T(8,128)(2,1)} async-done(((bf16[4,256,256]{2,1,0:T(8,128)(2,1)}), bf16[1,256,256]{2,1,0:T(8,128)(2,1)}) %reduce-scatter.19.cloned.1.call-update) | async-done | bytes 131088
  55.9 1.5 fusion.6
  57.4 15.4 %all-gather.1 = bf16[1024,256]{0,1:T(8,128)(2,1)S(1)} all-gather(bf16[256,256]{0,1:T(8,128)(2,1)S(1)} %fusion.6), channel_id=3, replica_groups=mesh['layer'=2,'prow'=4,'pcol'=4] {'prow'}, dimensions={0}, use_global_device_ids=true | all-gather | bytes 655360 | tf_op jit(solution)/shard_map/all_gather | solution.py:23
  74.0 1.9 fusion.1
  77.0 25.9 %reduce-scatter.21.cloned.1.call-done = bf16[1,256,256]{2,1,0:T(8,128)(2,1)} async-done(((bf16[4,256,256]{2,1,0:T(8,128)(2,1)}), bf16[1,256,256]{2,1,0:T(8,128)(2,1)}) %reduce-scatter.21.cloned.1.call-update) | async-done | bytes 131088
  102.9 1.5 fusion.39
  104.4 15.4 %all-gather.2 = bf16[1024,256]{0,1:T(8,128)(2,1)S(1)} all-gather(bf16[256,256]{0,1:T(8,128)(2,1)S(1)} %get-tuple-element.6), channel_id=4, replica_groups=mesh['layer'=2,'prow'=4,'pcol'=4] {'prow'}, dimensions={0}, use_global_device_ids=true | all-gather | bytes 655360 | tf_op jit(solution)/shard_map/all_gather | solution.py:23
  121.0 3.4 %fusion = bf16[4,256,256]{1,2,0:T(8,128)(2,1)} fusion(f32[4,4]{0,1:T(4,128)S(1)} %copy.34, bf16[4,256,256,1]{1,0,2,3:T(4,128)(2,1)} %bitcast.163, bf16[1,1,4,4,1,256,256]{6,5,4,3,2,1,0:T(8,128)(2,1)} %param.13), kind=kOutput, calls=%fused_computation.1 | convolution fusion | flops 538705920 | bytes 3145792 | tf_op jit(solution)/shard_map/bawk,akr->bawr/dot_general | solution.py:20
  124.4 2.1 copy.35
  126.6 26.0 %reduce-scatter.23.cloned.1.call-done = bf16[1,256,256]{2,1,0:T(8,128)(2,1)} async-done(((bf16[4,256,256]{2,1,0:T(8,128)(2,1)}), bf16[1,256,256]{2,1,0:T(8,128)(2,1)}) %reduce-scatter.23.cloned.1.call-update) | async-done | bytes 131088
  152.6 2.2 all_gather.25
  155.9 14.1 %all-gather.3 = bf16[1024,256]{0,1:T(8,128)(2,1)S(1)} all-gather(bf16[256,256]{0,1:T(8,128)(2,1)S(1)} %get-tuple-element.8), channel_id=5, replica_groups=mesh['layer'=2,'prow'=4,'pcol'=4] {'pcol'}, dimensions={0}, use_global_device_ids=true | all-gather | bytes 655360 | tf_op jit(solution)/shard_map/all_gather | solution.py:34
  171.1 3.4 %multiply_reduce_fusion.2 = bf16[256,4,256]{2,0,1:T(8,128)(2,1)} fusion(f32[4,4]{1,0:T(4,128)S(1)} %bitcast.171, bf16[4,256,256,1]{1,0,2,3:T(4,128)(2,1)} %bitcast.164, bf16[1,1,4,4,1,256,256]{6,5,4,3,2,1,0:T(8,128)(2,1)} %param.13), kind=kOutput, calls=%fused_computation.8 | convolution fusion | flops 538705920 | bytes 3145792 | tf_op jit(solution)/shard_map/bakw,bkr->bawr/dot_general | solution.py:31
  174.6 21.9 %reduce-scatter.13.cloned.1.call-done = bf16[1,256,256]{1,2,0:T(8,128)(2,1)} async-done(((bf16[4,256,256]{1,2,0:T(8,128)(2,1)}), bf16[1,256,256]{1,2,0:T(8,128)(2,1)}) %reduce-scatter.13.cloned.1.call-update) | async-done | bytes 131088 | tf_op jit(solution)/shard_map/reduce_scatter | solution.py:38
  197.8 12.0 %all-gather.4 = bf16[1024,256]{0,1:T(8,128)(2,1)S(1)} all-gather(bf16[256,256]{0,1:T(8,128)(2,1)S(1)} %fusion.7), channel_id=6, replica_groups=mesh['layer'=2,'prow'=4,'pcol'=4] {'pcol'}, dimensions={0}, use_global_device_ids=true | all-gather | bytes 655360 | tf_op jit(solution)/shard_map/all_gather | solution.py:34
  211.0 2.7 multiply_reduce_fusion.1
  213.8 19.4 %reduce-scatter.15.cloned.1.call-done = bf16[1,256,256]{1,2,0:T(8,128)(2,1)} async-done(((bf16[4,256,256]{1,2,0:T(8,128)(2,1)}), bf16[1,256,256]{1,2,0:T(8,128)(2,1)}) %reduce-scatter.15.cloned.1.call-update) | async-done | bytes 131088 | tf_op jit(solution)/shard_map/reduce_scatter | solution.py:38
  233.2 1.3 fusion.8
  234.5 12.1 %all-gather.5 = bf16[1024,256]{0,1:T(8,128)(2,1)S(1)} all-gather(bf16[256,256]{0,1:T(8,128)(2,1)S(1)} %fusion.8), channel_id=7, replica_groups=mesh['layer'=2,'prow'=4,'pcol'=4] {'pcol'}, dimensions={0}, use_global_device_ids=true | all-gather | bytes 655360 | tf_op jit(solution)/shard_map/all_gather | solution.py:34
  247.7 2.7 multiply_reduce_fusion
  251.3 18.6 %reduce-scatter.17.cloned.1.call-done = bf16[1,256,256]{1,2,0:T(8,128)(2,1)} async-done(((bf16[4,256,256]{1,2,0:T(8,128)(2,1)}), bf16[1,256,256]{1,2,0:T(8,128)(2,1)}) %reduce-scatter.17.cloned.1.call-update) | async-done | bytes 131088 | tf_op jit(solution)/shard_map/reduce_scatter | solution.py:38
  269.8 1.3 convolution_bitcast_fusion
  (46 shorter events, 14.2 us)
Async XLA Ops:
  7.2 19.8 %copy-start = (bf16[1,1,4,4,1,256,256]{6,5,4,3,2,1,0:T(8,128)(2,1)S(1)}, bf16[1,1,4,4,1,256,256]{6,5,4,3,2,1,0:T(8,128)(2,1)}, u32[]{:S(2)}) copy-start(bf16[1,1,4,4,1,256,256]{6,5,4,3,2,1,0:T(8,128)(2,1)} %param.10) | copy-start | bytes 6291460
  7.2 48.7 %reduce-scatter.19.cloned.1.call-start = ((), (), s32[]{:S(2)}) async-start(), calls=%async_computation.9 | async-start | bytes 655360
  27.0 29.0 %copy-start.1 = (f32[1,1,1,256,256]{4,3,2,1,0:T(8,128)S(1)}, f32[1,1,1,256,256]{4,3,2,1,0:T(8,128)}, u32[]{:S(2)}) copy-start(f32[1,1,1,256,256]{4,3,2,1,0:T(8,128)} %param.16) | copy-start | bytes 786436
  27.0 29.0 %copy-start.2 = (f32[1,1,1,256,256]{4,3,2,1,0:T(8,128)S(1)}, f32[1,1,1,256,256]{4,3,2,1,0:T(8,128)}, u32[]{:S(2)}) copy-start(f32[1,1,1,256,256]{4,3,2,1,0:T(8,128)} %param.18) | copy-start | bytes 786436
  28.9 74.0 %reduce-scatter.21.cloned.1.call-start = ((), (), s32[]{:S(2)}) async-start(), calls=%async_computation.10 | async-start | bytes 655360
  74.0 2.9 %copy-start.6 = (f32[1,1,4,4,1]{3,4,2,1,0:T(1,128)S(1)}, f32[1,1,4,4,1]{3,4,2,1,0:T(1,128)}, u32[]{:S(2)}) copy-start(f32[1,1,4,4,1]{3,4,2,1,0:T(1,128)} %param.14) | copy-start | bytes 196
  74.0 3.0 %copy-start.7 = (s32[1,1,4,4,1]{3,4,2,1,0:T(1,128)S(1)}, s32[1,1,4,4,1]{3,4,2,1,0:T(1,128)}, u32[]{:S(2)}) copy-start(s32[1,1,4,4,1]{3,4,2,1,0:T(1,128)} %param.15) | copy-start | bytes 196
  76.9 75.7 %reduce-scatter.23.cloned.1.call-start = ((), (), s32[]{:S(2)}) async-start(), calls=%async_computation.11 | async-start | bytes 655360
  124.4 30.4 %copy-start.4 = (f32[1,1,256,256]{3,2,1,0:T(8,128)S(1)}, f32[1,1,256,256]{3,2,1,0:T(8,128)}, u32[]{:S(2)}) copy-start(f32[1,1,256,256]{3,2,1,0:T(8,128)} %param.17) | copy-start | bytes 786436
  124.4 30.4 %copy-start.5 = (f32[1,1,256,256]{3,2,1,0:T(8,128)S(1)}, f32[1,1,256,256]{3,2,1,0:T(8,128)}, u32[]{:S(2)}) copy-start(f32[1,1,256,256]{3,2,1,0:T(8,128)} %param.19) | copy-start | bytes 786436
  126.6 70.0 %reduce-scatter.13.cloned.1.call-start = ((), (), s32[]{:S(2)}) async-start(), calls=%async_computation.6 | async-start | bytes 655360 | tf_op jit(solution)/shard_map/reduce_scatter | solution.py:38
  174.6 58.6 %reduce-scatter.15.cloned.1.call-start = ((), (), s32[]{:S(2)}) async-start(), calls=%async_computation.7 | async-start | bytes 655360 | tf_op jit(solution)/shard_map/reduce_scatter | solution.py:38
  211.0 22.1 %copy-start.3 = (bf16[1,256,256]{1,2,0:T(8,128)(2,1)S(1)}, bf16[1,256,256]{1,2,0:T(8,128)(2,1)}, u32[]{:S(2)}) copy-start(bf16[1,256,256]{1,2,0:T(8,128)(2,1)} %reduce-scatter.13.cloned.1.call-done) | copy-start | bytes 393220
  213.7 56.1 %reduce-scatter.17.cloned.1.call-start = ((), (), s32[]{:S(2)}) async-start(), calls=%async_computation.8 | async-start | bytes 655360 | tf_op jit(solution)/shard_map/reduce_scatter | solution.py:38
Sparse Core Ops, SparseCore 0:
  29.0 26.8 reduce-scatter.18
  77.0 25.8 reduce-scatter.20
  126.7 25.8 reduce-scatter.22
  174.7 21.8 reduce-scatter.12
  213.9 19.2 reduce-scatter.14
  250.6 19.2 reduce-scatter.16
